TPU v7x, 128 devices: a whole 4x4x4 slice. The times are simulated.
128 devices in a mesh: tok: 4 (over x), feat: 16 (over y_lo, z, core), row: 2 (over y_hi).
Axes of the slice: x: 4, y: 4 (y_hi: 2, y_lo: 2; y = y_hi * 2 + y_lo), z: 4, core: 2. Of those that a mesh axis runs over, the one named last changes fastest.
Arguments:
- quantized: bfloat16 [16384, 28672], P('tok', 'feat'), may hold values from -8 to 8
- exponents: int32 [16384, 224], P('tok', 'feat'), may hold values from -3 to 3
- weights: bfloat16 [8192, 28672], P(('tok', 'row'), 'feat'), may hold values from -6 to 6
- keep_mask: int32 [8192, 256], P(('tok', 'row')), may hold values from 0 to 1, as said below
Outputs:
- pruned: bfloat16 [8192, 28672], P(('tok', 'row'), 'feat')
Inputs may be any that keep to these rules, and one draw needn't show every extreme that they name: `keep_mask`: in every row each group of four consecutive columns holds exactly two ones.
All inputs are finite; a program needn't handle non-finite values.
Results may differ from a plain program's by a relative error of at most 0.0012.
Values may be sent and summed in bfloat16 or wider, within the bound.
A program may use at most 128 MiB of HBM per device.

v0:
```python
import jax
import jax.numpy as jnp
from jax import lax
from jax.sharding import PartitionSpec as P

PANEL = 256
QBLOCK = 128


def filled_up(lines, length):
    spare = -len(lines) % length
    return jnp.pad(lines, [(0, spare)] + [(0, 0)] * (lines.ndim - 1))


def spread(x, axis, root):
    lines = jnp.where(lax.axis_index(axis) == root, x, jnp.zeros_like(x)).reshape(
        -1, *x.shape[1:][-1:]
    )
    padded = filled_up(lines, lax.axis_size(axis))
    own = lax.psum_scatter(padded, axis, scatter_dimension=0, tiled=True)
    return lax.all_gather(own, axis, axis=0, tiled=True)[: len(lines)].reshape(x.shape)


def picked(x, axis, root):
    return lax.dynamic_index_in_dim(lax.all_gather(x, axis), root, 0, keepdims=False)


def matmul_high(left, right):
    return jnp.dot(left, right, precision=lax.Precision.HIGHEST)


def factor_small(block):
    size = block.shape[0]
    lower = jnp.zeros_like(block)
    for j in range(size):
        head = lower[j, :j]
        diag_value = jnp.sqrt(block[j, j] - jnp.sum(head * head))
        column = (block[j:, j] - matmul_high(lower[j:, :j], head)) / diag_value
        lower = lower.at[j:, j].set(column)
    ident = jnp.eye(size, dtype=block.dtype)
    inverse = jnp.zeros_like(block)
    for i in range(size):
        row_value = (ident[i] - matmul_high(lower[i, :i], inverse[:i, :])) / lower[i, i]
        inverse = inverse.at[i].set(row_value)
    return (lower, inverse)


def factor_with_inverse(block):
    size = block.shape[0]
    if size <= 16:
        return factor_small(block)
    half = size // 2
    upper_lower, upper_inverse = factor_with_inverse(block[:half, :half])
    below = matmul_high(block[half:, :half], upper_inverse.T)
    rest = block[half:, half:] - matmul_high(below, below.T)
    rest_lower, rest_inverse = factor_with_inverse(rest)
    zeros_top = jnp.zeros((half, size - half), block.dtype)
    lower = jnp.concatenate(
        [
            jnp.concatenate([upper_lower, zeros_top], axis=1),
            jnp.concatenate([below, rest_lower], axis=1),
        ],
        axis=0,
    )
    cross = -matmul_high(rest_inverse, matmul_high(below, upper_inverse))
    inverse = jnp.concatenate(
        [
            jnp.concatenate([upper_inverse, zeros_top], axis=1),
            jnp.concatenate([cross, rest_inverse], axis=1),
        ],
        axis=0,
    )
    return (lower, inverse)


def solve_coeffs(diag_block, panel_weights, keep_mask):
    factor, factor_inv = factor_with_inverse(diag_block)
    pruned_error = panel_weights * (1.0 - keep_mask.astype(jnp.float32))
    return matmul_high(matmul_high(pruned_error, factor_inv.T), factor_inv)


def shards(quantized, exponents, weights, keep_mask):
    feat_cols = quantized.shape[1]
    panel_weights = weights[:, :PANEL]
    tok_rows = quantized.shape[0]
    scales = jnp.exp2(exponents.astype(jnp.float32)).astype(jnp.bfloat16)
    activations = (
        quantized.reshape(tok_rows, feat_cols // QBLOCK, QBLOCK) * scales[:, :, None]
    ).reshape(tok_rows, feat_cols)
    panel_acts = spread(activations[:, :PANEL], "feat", 0)
    partial_gram = lax.dot_general(
        activations, panel_acts, (((0,), (0,)), ((), ())), preferred_element_type=jnp.float32
    )
    hessian_panel = lax.psum(partial_gram, "tok")
    head_block = hessian_panel[:PANEL]
    damping = 0.01 * jnp.mean(jnp.diagonal(head_block))
    diag_block = head_block + damping * jnp.eye(PANEL, dtype=jnp.float32)
    own_coeffs = solve_coeffs(diag_block, panel_weights.astype(jnp.float32), keep_mask)
    coefficients = picked(own_coeffs, "feat", 0)
    update = jnp.dot(coefficients, hessian_panel.T, precision=lax.Precision.HIGHEST)
    columns = lax.axis_index("feat") * feat_cols + jnp.arange(feat_cols, dtype=jnp.int32)[None, :]
    weights_float = weights.astype(jnp.float32)
    mask_padded = (
        jnp.ones((weights.shape[0], feat_cols), jnp.float32)
        .at[:, :PANEL]
        .set(keep_mask.astype(jnp.float32))
    )
    result = jnp.where(columns < PANEL, weights_float * mask_padded, weights_float + update)
    return result.astype(jnp.bfloat16)


def solution(mesh):
    placed = (
        P("tok", "feat"),
        P("tok", "feat"),
        P(("tok", "row"), "feat"),
        P(("tok", "row"), None),
    )
    return jax.shard_map(
        shards, mesh=mesh, in_specs=placed, out_specs=P(("tok", "row"), "feat"), check_vma=False
    )
```

profile of v0, /device:TPU:104, one launch (start us, length us, event | category | flops | bytes accessed | tf_op | source)
XLA Modules:
  0.0 1244.2 jit_solution(14887447826673966476)
XLA Ops:
  7.5 19.8 %copy.230 = bf16[4096,1792]{0,1:T(8,128)(2,1)} copy(bf16[4096,1792]{1,0:T(8,128)(2,1)} %param.1030) | data formatting | bytes 29360128 | tf_op args[0]
  27.3 7.4 bitcast_multiply_fusion
  34.7 5.2 copy-done
  39.9 1.5 slice_select_fusion
  41.5 61.3 %reduce-scatter.2.cloned.1.call-done = bf16[256,256]{0,1:T(8,128)(2,1)} async-done(((bf16[4096,256]{0,1:T(8,128)(2,1)}), bf16[256,256]{0,1:T(8,128)(2,1)}) %reduce-scatter.2.cloned.1.call-update) | async-done | bytes 131088 | tf_op jit(solution)/shard_map/reduce_scatter | solution.py:20
  102.8 39.8 %all-gather.4.cloned.1.call-done = bf16[4096,256]{0,1:T(8,128)(2,1)} async-done(((bf16[256,256]{0,1:T(8,128)(2,1)}), bf16[4096,256]{0,1:T(8,128)(2,1)}) %all-gather.4.cloned.1.call-update) | async-done | bytes 2097168 | tf_op jit(solution)/shard_map/all_gather | solution.py:21
  142.6 11.1 fusion.2581
  154.5 55.4 %all-reduce.50.cloned.1.call-done = f32[1792,256]{1,0:T(8,128)} async-done(((f32[1792,256]{1,0:T(8,128)}), f32[1792,256]{1,0:T(8,128)}) %all-reduce.50.cloned.1.call-update) | async-done | bytes 1835024 | tf_op jit(solution)/shard_map/psum | solution.py:94
  210.9 2.3 gather_fusion
  257.1 1.9 subtract_divide_fusion.15
  259.0 1.4 fusion.1206
  260.5 1.5 fusion.646
  262.0 1.4 fusion.649
  263.4 1.5 fusion.652
  264.9 1.5 fusion.655
  266.4 1.5 fusion.658
  267.9 1.5 fusion.661
  269.4 1.5 fusion.223
  270.9 1.4 fusion.225
  272.3 1.5 fusion.227
  273.9 1.4 fusion.229
  275.3 1.5 fusion.231
  322.0 2.6 subtract_divide_fusion.14
  326.1 1.5 fusion.682
  327.5 1.4 fusion.685
  329.0 1.5 fusion.688
  330.5 1.4 fusion.691
  332.0 1.5 fusion.694
  333.5 1.4 fusion.697
  334.9 1.5 fusion.249
  336.4 1.4 fusion.251
  337.8 1.4 fusion.253
  339.3 1.4 fusion.255
  340.7 1.4 fusion.257
  387.6 2.6 subtract_divide_fusion.13
  390.2 1.4 fusion.1216
  391.7 1.5 fusion.718
  393.2 1.4 fusion.721
  394.6 1.5 fusion.724
  396.1 1.5 fusion.727
  397.6 1.5 fusion.730
  399.1 1.5 fusion.733
  400.6 1.5 fusion.275
  402.1 1.4 fusion.277
  403.6 1.5 fusion.279
  405.1 1.4 fusion.281
  406.5 1.5 fusion.283
  453.4 1.9 subtract_divide_fusion.12
  509.1 1.8 subtract_divide_fusion.11
  564.4 1.8 subtract_divide_fusion.10
  619.8 1.8 subtract_divide_fusion.9
  675.2 1.8 subtract_divide_fusion.8
  731.4 1.8 subtract_divide_fusion.7
  786.9 1.8 subtract_divide_fusion.6
  842.3 1.8 subtract_divide_fusion.5
  897.7 1.8 subtract_divide_fusion.4
  953.5 1.8 subtract_divide_fusion.3
  1008.8 1.8 subtract_divide_fusion.2
  1064.3 1.8 subtract_divide_fusion.1
  1118.1 1.8 subtract_divide_fusion
  1132.0 2.1 fusion.1283
  1134.1 2.0 fusion.2548
  1137.6 89.3 %all-gather.6.cloned.1.call-done = f32[16384,256]{1,0:T(8,128)} async-done(((f32[1024,256]{1,0:T(8,128)}), f32[16384,256]{1,0:T(8,128)}) %all-gather.6.cloned.1.call-update) | async-done | bytes 16777232 | tf_op jit(solution)/shard_map/all_gather | solution.py:25
  1226.9 10.3 fusion.1
  (1716 shorter events, 486.2 us)
Async XLA Ops:
  6.5 96.2 %reduce-scatter.2.cloned.1.call-start = ((), (), s32[]{:S(2)}) async-start(), calls=%async_computation.1 | async-start | bytes 2228224 | tf_op jit(solution)/shard_map/reduce_scatter | solution.py:20
  34.7 5.2 copy-start
  41.4 101.2 %all-gather.4.cloned.1.call-start = ((), (), s32[]{:S(2)}) async-start(), calls=%async_computation.2 | async-start | bytes 2228224 | tf_op jit(solution)/shard_map/all_gather | solution.py:21
  102.8 107.2 %all-reduce.50.cloned.1.call-start = ((), (), s32[]{:S(2)}) async-start(), calls=%async_computation.3 | async-start | bytes 3670016 | tf_op jit(solution)/shard_map/psum | solution.py:94
  153.8 1073.1 %all-gather.6.cloned.1.call-start = ((), (), s32[]{:S(2)}) async-start(), calls=%async_computation.4 | async-start | bytes 17825792 | tf_op jit(solution)/shard_map/all_gather | solution.py:25
  154.5 104.5 %copy-start.2 = (f32[16,16]{1,0:T(8,128)}, f32[16,16]{1,0:T(8,128)S(1)}, u32[]{:S(2)}) copy-start(f32[16,16]{1,0:T(8,128)S(1)} %fusion.1627) | copy-start | bytes 3076
  254.4 4.6 copy-start.4
  260.5 192.9 %copy-start.3 = (f32[16,16]{1,0:T(8,128)S(1)}, f32[16,16]{1,0:T(8,128)}, u32[]{:S(2)}) copy-start(f32[16,16]{1,0:T(8,128)} %copy-done.2) | copy-start | bytes 3076
  384.9 5.3 copy-start.5
  904.2 227.7 %copy-start.1 = (s32[1024,256]{1,0:T(8,128)S(1)}, s32[1024,256]{1,0:T(8,128)}, u32[]{:S(2)}) copy-start(s32[1024,256]{1,0:T(8,128)} %param.1033) | copy-start | bytes 3145732
Sparse Core Ops, SparseCore 0:
  41.5 61.1 reduce-scatter.1
  104.4 38.2 all-gather.3
  153.9 55.9 all-reduce.49
  1136.3 90.6 all-gather.5
where the time goes:
time: 1260 us; the launch traced here: 1240 us
  between operations  369 us (29%)
  waiting for transfers between devices  246 us (20%)
  matrix products  242 us (19%)
  other arithmetic  208 us (17%)
  local copies, waits for them, and re-layouts  180 us (14%)
    dot_general x494, matrix products, matmul_high(): return jnp.dot(left, right, precision=lax.Precision.HIGHEST)  220 us
    reduce_sum x224, other arithmetic, factor_small(): diag_value = jnp.sqrt(block[j, j] - jnp.sum(head * head))  143 us
    all_gather x1, waiting for transfers between devices, picked(): lax.all_gather(x, axis)  89.3 us
    reduce_scatter x1, waiting for transfers between devices, spread(): own = lax.psum_scatter(padded, axis, scatter_dimension=0, tiled=True)  61.3 us
    psum x1, waiting for transfers between devices, shards(): hessian_panel = lax.psum(partial_gram, 'tok')  55.4 us
    scatter x240, local copies, waits for them, and re-layouts, factor_small(): lower = lower.at[j:, j].set(column)  53.6 us
    slice x224, local copies, waits for them, and re-layouts, factor_small(): column = (block[j:, j] - matmul_high(lower[j:, :j], head)) / diag_value  49.4 us
    all_gather x1, waiting for transfers between devices, spread(): lax.all_gather(own, axis, axis=0, tiled=True)[:len(lines)].reshape(x.shape)  39.8 us
  transfers between devices with their start and end apart: 4, of which 4 were waited for; matrix products, arithmetic and copies ran while one was open for 0% of the time, Pallas kernels for 0%

commit v1 on v0

v1 whole, which is shorter than its diff:
```python
import functools

import jax
import jax.numpy as jnp
from jax import lax
from jax.experimental import pallas as pl
from jax.experimental.pallas import tpu as pltpu
from jax.sharding import PartitionSpec as P

PANEL = 256
QBLOCK = 128
CHUNK = 256
SQUARINGS = 18
POLISH = 2
MESH = pl.DeviceIdType.MESH
F32 = jnp.float32
BF16 = jnp.bfloat16


def high(left, right):
    return jnp.dot(left, right, precision=lax.Precision.HIGHEST, preferred_element_type=F32)


def split(value):
    top = value.astype(BF16)
    return top, (value - top.astype(F32)).astype(BF16)


def exchange_kernel(
    sizes,
    panel_ref, error_ref, quant_ref, scale_ref,
    hess_ref, inv_ref, error_out,
    acts, quant, part, summed, diag_part, diag, square, inverse, scaled,
    load_sem, quant_sem, arrive, send_z, send_y, send_c,
    diag_send, diag_recv, half_send, half_recv,
    err_send, err_recv,
    red_send, red_recv, all_send, all_recv, row_send, row_recv,
):
    n_chunks, n_pairs, n_err, width, n_feat, n_tok = sizes
    tok, feat, row = lax.axis_index("tok"), lax.axis_index("feat"), lax.axis_index("row")
    y_lo, z, core = feat // 8, (feat // 2) % 4, feat % 2
    strip = PANEL // n_tok
    n_quant = n_feat * width

    def at(t, y, zz, c, r):
        return (t, (y * 4 + zz) * 2 + c, r)

    z_up, z_down = (z + 1) % 4, (z + 3) % 4
    z_next = core * z_down + (1 - core) * z_up
    hops = core * ((4 - z) % 4) + (1 - core) * z
    cross_row = core * (1 - row) + (1 - core) * row
    to_z = at(tok, y_lo, z_next, core, row)
    to_y = at(tok, 1 - y_lo, z, core, cross_row)
    to_y_same = at(tok, 1 - y_lo, z, core, row)
    to_c = at(tok, y_lo, z, 1 - core, row)
    to_row = (tok, feat, 1 - row)
    peers = [((tok + k) % n_tok, feat, row) for k in range(1, n_tok)]
    greeted = [
        at(tok, y_lo, z_up, core, row), at(tok, y_lo, z_down, core, row),
        at(tok, 1 - y_lo, z, core, 0), at(tok, 1 - y_lo, z, core, 1),
        to_c, to_row,
    ] + peers
    even_y = y_lo == 0
    is_source = feat == 0
    is_twin = feat == 1
    can_z = jnp.logical_and(even_y, hops < 3)
    not_twin = feat != 1

    def own(j):
        return 2 * j + core

    def other(j):
        return 2 * j + 1 - core

    def rows_of(c, size=CHUNK):
        return pl.ds(pl.multiple_of(c * size, size), size)

    def load(c):
        return pltpu.make_async_copy(panel_ref.at[rows_of(c)], acts.at[rows_of(c)], arrive.at[c])

    def send(c, target, sem):
        return pltpu.make_async_remote_copy(
            src_ref=acts.at[rows_of(c)], dst_ref=acts.at[rows_of(c)], send_sem=sem.at[c],
            recv_sem=arrive.at[c], device_id=target, device_id_type=MESH)

    def quant_load(c):
        cols = pl.ds(pl.multiple_of(row * n_quant, 128), n_quant)
        return pltpu.make_async_copy(
            quant_ref.at[rows_of(c), cols], quant.at[rows_of(c)], quant_sem.at[c])

    @pl.when(is_source)
    def _():
        for c in range(n_chunks):
            load(c).start()
        pltpu.make_async_copy(error_ref, error_out, load_sem.at[0]).start()

    for c in range(n_chunks):
        quant_load(c).start()

    barrier = pltpu.get_barrier_semaphore()
    for device in greeted:
        pl.semaphore_signal(barrier, inc=1, device_id=device, device_id_type=MESH)
    pl.semaphore_wait(barrier, len(greeted))

    def forward(c):
        @pl.when(can_z)
        def _():
            send(c, to_z, send_z).start()

        @pl.when(even_y)
        def _():
            send(c, to_y, send_y).start()

        @pl.when(not_twin)
        def _():
            send(c, to_c, send_c).start()

    @pl.when(is_source)
    def _():
        def body(j, carry):
            load(own(j)).wait()
            forward(own(j))
            load(other(j)).wait()
            send(other(j), to_c, send_c).start()
            return carry

        lax.fori_loop(0, n_pairs, body, 0)

        def gram(c, carry):
            block = acts[rows_of(c), :]
            term = lax.dot_general(block, block, (((0,), (0,)), ((), ())), preferred_element_type=F32)

            @pl.when(c == 0)
            def _():
                diag_part[tok] = term

            @pl.when(c > 0)
            def _():
                diag_part[tok] += term

            return carry

        lax.fori_loop(0, n_chunks, gram, 0)
        for k, device in enumerate(peers):
            diag_copy(diag_part, diag_send, diag_recv, tok, k, device).start()

    def accumulate(c, first):
        quant_load(c).wait()
        scales = scale_ref[rows_of(c), :]
        blocks = []
        for b in range(n_quant // QBLOCK):
            scale = jnp.broadcast_to(scales[:, b:b + 1], (CHUNK, QBLOCK)).astype(BF16)
            blocks.append(quant[rows_of(c), b * QBLOCK:(b + 1) * QBLOCK] * scale)
        value = jnp.concatenate(blocks, axis=1)
        term = lax.dot_general(
            acts[rows_of(c), :], value, (((0,), (0,)), ((), ())), preferred_element_type=F32)
        for i in range(n_feat):
            piece = term[:, i * width:(i + 1) * width]
            if first:
                part[i] = piece
            else:
                part[i] += piece

    def pair(j, first):
        @pl.when(jnp.logical_not(is_source))
        def _():
            send(own(j), to_c, send_c).wait_recv()
            forward(own(j))

        accumulate(own(j), first)

        @pl.when(jnp.logical_not(is_source))
        def _():
            send(other(j), to_c, send_c).wait_recv()

        accumulate(other(j), False)

    pair(0, True)

    def later(j, carry):
        pair(j, False)
        return carry

    lax.fori_loop(1, n_pairs, later, 0)

    def red_copy(i, k, device):
        dest = device[0]
        return pltpu.make_async_remote_copy(
            src_ref=part.at[i, rows_of(dest, strip)], dst_ref=summed.at[i, tok],
            send_sem=red_send.at[i, k], recv_sem=red_recv.at[i, n_tok - 2 - k],
            device_id=device, device_id_type=MESH)

    for i in range(n_feat):
        for k, device in enumerate(peers):
            red_copy(i, k, device).start()

    def half_copy(h, target, slot):
        return pltpu.make_async_remote_copy(
            src_ref=diag.at[rows_of(h, PANEL // 2)], dst_ref=diag.at[rows_of(h, PANEL // 2)],
            send_sem=half_send.at[slot], recv_sem=half_recv.at[h],
            device_id=target, device_id_type=MESH)

    def err_copy(c, target, slot):
        return pltpu.make_async_remote_copy(
            src_ref=error_out.at[rows_of(c)], dst_ref=error_out.at[rows_of(c)],
            send_sem=err_send.at[slot, c], recv_sem=err_recv.at[c],
            device_id=target, device_id_type=MESH)

    def half_forward():
        @pl.when(can_z)
        def _():
            half_copy(core, to_z, 0).start()

        @pl.when(even_y)
        def _():
            half_copy(core, to_y, 1).start()

        @pl.when(not_twin)
        def _():
            half_copy(core, to_c, 2).start()

    def err_forward(c):
        @pl.when(can_z)
        def _():
            err_copy(c, to_z, 0).start()

        @pl.when(even_y)
        def _():
            err_copy(c, to_y_same, 1).start()

        @pl.when(not_twin)
        def _():
            err_copy(c, to_c, 2).start()

    @pl.when(is_source)
    def _():
        for k, device in enumerate(peers):
            diag_copy(diag_part, diag_send, diag_recv, tok, k, device).wait_recv()
        total = diag_part[0]
        for t in range(1, n_tok):
            total = total + diag_part[t]
        diag[...] = total
        half_forward()
        half_copy(1, to_c, 3).start()
        pltpu.make_async_copy(error_ref, error_out, load_sem.at[0]).wait()
        for j in range(n_err // 2):
            err_forward(own(j))
            err_copy(other(j), to_c, 2).start()

    @pl.when(jnp.logical_not(is_source))
    def _():
        half_copy(core, to_c, 0).wait_recv()
        half_forward()
        for j in range(n_err // 2):
            err_copy(own(j), to_c, 0).wait_recv()
            err_forward(own(j))
        half_copy(1 - core, to_c, 0).wait_recv()

    eye = (lax.broadcasted_iota(jnp.int32, (PANEL, PANEL), 0)
           == lax.broadcasted_iota(jnp.int32, (PANEL, PANEL), 1)).astype(F32)
    block = diag[...]
    trace = jnp.sum(jnp.sum(block * eye, axis=1, keepdims=True), axis=0, keepdims=True)
    damped = block + (0.01 / PANEL) * trace * eye
    shrink = 1.0 / (1.01 * trace)
    scaled[...] = damped * shrink
    square[...] = eye - scaled[...]
    inverse[...] = eye + square[...]

    def double(s, carry):
        r = square[...]
        r2 = high(r, r)
        square[...] = r2
        x = inverse[...]
        inverse[...] = x + high(x, r2)
        return carry

    lax.fori_loop(0, SQUARINGS, double, 0)

    def polish(s, carry):
        x = inverse[...]
        inverse[...] = x + high(x, eye - high(scaled[...], x))
        return carry

    lax.fori_loop(0, POLISH, polish, 0)
    inv_ref[...] = inverse[...] * shrink

    def all_copy(i, k, device):
        piece = hess_ref.at[row, i, rows_of(tok, strip)]
        return pltpu.make_async_remote_copy(
            src_ref=piece, dst_ref=piece, send_sem=all_send.at[i, k],
            recv_sem=all_recv.at[i, n_tok - 2 - k], device_id=device, device_id_type=MESH)

    def row_copy(i, k):
        owner = (tok + k) % n_tok
        piece = hess_ref.at[row, i, rows_of(owner, strip)]
        return pltpu.make_async_remote_copy(
            src_ref=piece, dst_ref=piece, send_sem=row_send.at[i, k],
            recv_sem=row_recv.at[i, k], device_id=to_row, device_id_type=MESH)

    for i in range(n_feat):
        for k, device in enumerate(peers):
            red_copy(i, k, device).wait_recv()
        mine = part[i, rows_of(tok, strip), :]
        for k in range(1, n_tok):
            mine = mine + summed[i, (tok + k) % n_tok]
        hess_ref[row, i, rows_of(tok, strip), :] = mine
        for k, device in enumerate(peers):
            all_copy(i, k, device).start()
        row_copy(i, 0).start()
    for i in range(n_feat):
        for k, device in enumerate(peers):
            all_copy(i, n_tok - 2 - k, device).wait_recv()
            row_copy(i, k + 1).start()

    for i in range(n_feat):
        for k in range(n_tok):
            row_copy(i, k).wait_recv()
    for i in range(n_feat):
        for k, device in enumerate(peers):
            red_copy(i, k, device).wait_send()
            all_copy(i, k, device).wait_send()
        for k in range(n_tok):
            row_copy(i, k).wait_send()

    @pl.when(jnp.logical_not(is_source))
    def _():
        for j in range(n_err // 2):
            err_copy(other(j), to_c, 0).wait_recv()

    def drain(j, carry):
        c = own(j)

        @pl.when(can_z)
        def _():
            send(c, to_z, send_z).wait_send()

        @pl.when(even_y)
        def _():
            send(c, to_y, send_y).wait_send()

        @pl.when(not_twin)
        def _():
            send(c, to_c, send_c).wait_send()

        @pl.when(is_source)
        def _():
            send(other(j), to_c, send_c).wait_send()

        return carry

    lax.fori_loop(0, n_pairs, drain, 0)

    @pl.when(can_z)
    def _():
        half_copy(core, to_z, 0).wait_send()
        for j in range(n_err // 2):
            err_copy(own(j), to_z, 0).wait_send()

    @pl.when(even_y)
    def _():
        half_copy(core, to_y, 1).wait_send()
        for j in range(n_err // 2):
            err_copy(own(j), to_y_same, 1).wait_send()

    @pl.when(not_twin)
    def _():
        half_copy(core, to_c, 2).wait_send()
        for j in range(n_err // 2):
            err_copy(own(j), to_c, 2).wait_send()

    @pl.when(is_source)
    def _():
        half_copy(1, to_c, 3).wait_send()
        for j in range(n_err // 2):
            err_copy(other(j), to_c, 2).wait_send()
        for k, device in enumerate(peers):
            diag_copy(diag_part, diag_send, diag_recv, tok, k, device).wait_send()


def diag_copy(diag_part, send_sem, recv_sem, tok, k, device):
    n = diag_part.shape[0]
    return pltpu.make_async_remote_copy(
        src_ref=diag_part.at[tok], dst_ref=diag_part.at[tok], send_sem=send_sem.at[k],
        recv_sem=recv_sem.at[n - 2 - k], device_id=device, device_id_type=MESH)


def exchange(panel, error, quantized, scales):
    tokens, columns = quantized.shape
    n_tok = lax.axis_size("tok")
    n_quant = columns // lax.axis_size("row")
    width = 128
    n_feat = n_quant // width
    n_chunks = tokens // CHUNK
    n_err = error.shape[0] // CHUNK
    strip = PANEL // n_tok
    sizes = (n_chunks, n_chunks // 2, n_err, width, n_feat, n_tok)
    dma = pltpu.SemaphoreType.DMA
    vmem = pl.BlockSpec(memory_space=pltpu.VMEM)
    hbm = pl.BlockSpec(memory_space=pl.ANY)
    return pl.pallas_call(
        functools.partial(exchange_kernel, sizes),
        out_shape=(
            jax.ShapeDtypeStruct((2, n_feat, PANEL, width), F32),
            jax.ShapeDtypeStruct((PANEL, PANEL), F32),
            jax.ShapeDtypeStruct(error.shape, BF16),
        ),
        in_specs=[hbm, hbm, hbm, vmem],
        out_specs=(vmem, vmem, vmem),
        scratch_shapes=[
            pltpu.VMEM((tokens, PANEL), BF16),
            pltpu.VMEM((tokens, n_quant), BF16),
            pltpu.VMEM((n_feat, PANEL, width), F32),
            pltpu.VMEM((n_feat, n_tok, strip, width), F32),
            pltpu.VMEM((n_tok, PANEL, PANEL), F32),
            pltpu.VMEM((PANEL, PANEL), F32),
            pltpu.VMEM((PANEL, PANEL), F32),
            pltpu.VMEM((PANEL, PANEL), F32),
            pltpu.VMEM((PANEL, PANEL), F32),
            dma((1,)), dma((n_chunks,)), dma((n_chunks,)),
            dma((n_chunks,)), dma((n_chunks,)), dma((n_chunks,)),
            dma((n_tok - 1,)), dma((n_tok - 1,)), dma((4,)), dma((2,)),
            dma((3, n_err)), dma((n_err,)),
            dma((n_feat, n_tok - 1)), dma((n_feat, n_tok - 1)),
            dma((n_feat, n_tok - 1)), dma((n_feat, n_tok - 1)),
            dma((n_feat, n_tok)), dma((n_feat, n_tok)),
        ],
        compiler_params=pltpu.CompilerParams(
            collective_id=0, has_side_effects=True, vmem_limit_bytes=60 * 1024 * 1024),
        name="exchange",
    )(panel, error, quantized, scales)


def update_kernel(feat_ref, hess_ref, inv_ref, error_ref, weights_ref, out_ref, product):
    n_rows, n_feat, _, width = hess_ref.shape

    @pl.when(pl.program_id(0) == 0)
    def _():
        top, low = split(inv_ref[...])
        for r in range(n_rows):
            for i in range(n_feat):
                h_top, h_low = split(hess_ref[r, i])
                value = (jnp.dot(top, h_top, preferred_element_type=F32)
                         + jnp.dot(top, h_low, preferred_element_type=F32)
                         + jnp.dot(low, h_top, preferred_element_type=F32))
                w_top, w_low = split(value)
                cols = pl.ds((r * n_feat + i) * width, width)
                product[:PANEL, cols] = w_top
                product[PANEL:, cols] = w_low

    error = error_ref[...]
    both = jnp.concatenate([error, error], axis=1)
    update = jnp.dot(both, product[...], preferred_element_type=F32)
    out_ref[...] = (weights_ref[...].astype(F32) + update).astype(BF16)

    @pl.when(feat_ref[0] == 0)
    def _():
        out_ref[:, :PANEL] = weights_ref[:, :PANEL] - error


def apply_update(feat, hess, inv, error, weights, tile=128):
    rows, columns = weights.shape
    return pl.pallas_call(
        update_kernel,
        grid=(rows // tile,),
        out_shape=jax.ShapeDtypeStruct(weights.shape, BF16),
        in_specs=[
            pl.BlockSpec(memory_space=pltpu.SMEM),
            pl.BlockSpec(memory_space=pltpu.VMEM),
            pl.BlockSpec(memory_space=pltpu.VMEM),
            pl.BlockSpec((tile, PANEL), lambda g: (g, 0)),
            pl.BlockSpec((tile, columns), lambda g: (g, 0)),
        ],
        out_specs=pl.BlockSpec((tile, columns), lambda g: (g, 0)),
        scratch_shapes=[pltpu.VMEM((2 * PANEL, columns), BF16)],
        name="update",
    )(feat, hess, inv, error, weights)


def shards(quantized, exponents, weights, keep_mask):
    tokens = quantized.shape[0]
    blocks = exponents.shape[1]
    scales = jnp.exp2(exponents.astype(F32))
    own = PANEL // QBLOCK
    panel = (
        quantized[:, :PANEL].reshape(tokens, own, QBLOCK)
        * scales[:, :own].astype(BF16)[:, :, None]
    ).reshape(tokens, PANEL)
    half = blocks // lax.axis_size("row")
    row_scales = lax.dynamic_slice_in_dim(scales, lax.axis_index("row") * half, half, 1)
    error = jnp.where(keep_mask == 0, weights[:, :PANEL], jnp.zeros((), BF16))
    hess, inv, error = exchange(panel, error, quantized, row_scales)
    feat = lax.axis_index("feat").astype(jnp.int32).reshape(1)
    return apply_update(feat, hess, inv, error, weights)


def solution(mesh):
    placed = (
        P("tok", "feat"),
        P("tok", "feat"),
        P(("tok", "row"), "feat"),
        P(("tok", "row"), None),
    )
    return jax.shard_map(
        shards, mesh=mesh, in_specs=placed, out_specs=P(("tok", "row"), "feat"), check_vma=False
    )
```

time: 1260 us -> 171 us (0.14); the launches traced: 1240 us -> 169 us
  between operations: 369 us -> 0.04 us
  waiting for transfers between devices: 246 us -> 0 us
  matrix products: 242 us -> 0 us
  other arithmetic: 208 us -> 6.46 us
  local copies, waits for them, and re-layouts: 180 us -> 14.2 us
  Pallas kernels: 0 us -> 149 us
    dot_general x496 -> x0, matrix products: 242 us -> none  [the longest x494 220 us: matmul_high(): return jnp.dot(left, right, precision=lax.Precision.HIGHEST)]
    pallas_call x0 -> x2, Pallas kernels: none -> 149 us  [the longest x1 139 us: exchange(): pl.pallas_call(functools.partial(exchange_kernel, sizes), out_shape=(jax....]
    reduce_sum x225 -> x0, other arithmetic: 143 us -> none  [the longest x224 143 us: factor_small(): diag_value = jnp.sqrt(block[j, j] - jnp.sum(head * head))]
    all_gather x2 -> x0, waiting for transfers between devices: 129 us -> none  [the longest x1 89.3 us: picked(): lax.all_gather(x, axis)]
    slice x257 -> x2, local copies, waits for them, and re-layouts: 70.4 us -> 0.53 us  [shards(): scales[:, :own].astype(BF16)[:, :, None]]
    scatter x496 -> x0, local copies, waits for them, and re-layouts: 62 us -> none  [the longest x240 53.6 us: factor_small(): lower = lower.at[j:, j].set(column)]
    reduce_scatter x1 -> x0, waiting for transfers between devices: 61.3 us -> none  [spread(): own = lax.psum_scatter(padded, axis, scatter_dimension=0, tiled=True)]
    psum x1 -> x0, waiting for transfers between devices: 55.4 us -> none  [shards(): hessian_panel = lax.psum(partial_gram, 'tok')]
  transfers between devices with their start and end apart: 4 -> 0, of which waited for: 4 -> 0; matrix products, arithmetic and copies ran while one was open for 0% -> 0% of each run, Pallas kernels for 0% -> 0%
where the time goes in v1:
time: 171 us; the launch traced here: 169 us
  Pallas kernels  149 us (87%)
  local copies, waits for them, and re-layouts  14.2 us (8%)
  other arithmetic  6.46 us (4%)
    pallas_call x1, Pallas kernels, exchange(): pl.pallas_call(functools.partial(exchange_kernel, sizes), out_shape=(jax....  139 us
    mul x1, local copies, waits for them, and re-layouts, shards(): quantized[:, :PANEL].reshape(tokens, own, QBLOCK)  11.6 us
    pallas_call x1, Pallas kernels, apply_update(): pl.pallas_call(update_kernel, grid=(rows // tile,), out_shape=jax.ShapeDt...  10.1 us

profile of v1, /device:TPU:104, one launch (start us, length us, event | category | flops | bytes accessed | tf_op | source)
XLA Modules:
  0.0 169.3 jit_solution(10952824517546752989)
XLA Ops:
  0.0 1.0 multiply_exponential_fusion
  1.1 2.3 %compare_select_fusion.error_ref = bf16[1024,256]{1,0:T(8,128)(2,1)} fusion(s32[1024,256]{1,0:T(8,128)} %param.7, bf16[1024,1792]{1,0:T(8,128)(2,1)} %weights_ref.1), kind=kLoop, calls=%fused_computation.1 | loop fusion | flops 524288 | bytes 2097152 | tf_op jit(solution)/shard_map/jit(_where)/select_n | solution.py:490
  3.3 0.5 copy.7
  3.9 11.6 %mul.14 = bf16[4096,2,128]{2,1,0:T(2,128)(2,1)S(1)} broadcast(bf16[4096,2]{1,0:T(8,128)(2,1)S(1)} %copy.7), dimensions={0,1} | broadcast | bytes 2113536 | tf_op jit(solution)/shard_map/mul | solution.py:485
  15.5 3.2 %bitcast_multiply_fusion.panel_ref = bf16[4096,256]{1,0:T(8,128)(2,1)} fusion(bf16[512,8,2,128]{3,2,1,0:T(2,128)(2,1)S(1)} %bitcast.4, bf16[4096,1792]{1,0:T(8,128)(2,1)} %quant_ref.1), kind=kLoop, calls=%fused_computation | loop fusion | flops 1048576 | bytes 6291456 | tf_op jit(solution)/shard_map/mul | solution.py:485
  18.7 2.0 %copy.9.scale_ref = f32[4096,7]{1,0:T(8,128)} copy(f32[4096,7]{0,1:T(8,128)S(1)} %constant_dynamic-slice_fusion) | data formatting | bytes 229376
  20.7 138.5 %exchange.1 = (f32[2,7,256,128]{3,2,1,0:T(8,128)}, f32[256,256]{1,0:T(8,128)}, bf16[1024,256]{1,0:T(8,128)(2,1)}) custom-call(bf16[4096,256]{1,0:T(8,128)(2,1)} %bitcast_multiply_fusion.panel_ref, bf16[1024,256]{1,0:T(8,128)(2,1)} %compare_select_fusion.error_ref, bf16[4096,1792]{1,0:T(8,128)(2,1)} %quant_ref.1, f32[4096,7]{1,0:T(8,128)} %copy.9.scale_ref), custom_call_target="tpu_custom_call" | custom-call | tf_op jit(solution)/shard_map/exchange/pallas_call | solution.py:400
  159.2 10.1 %update.1 = bf16[1024,1792]{1,0:T(8,128)(2,1)} custom-call(s32[1]{0:T(128)} %bitcast.feat_ref, f32[2,7,256,128]{3,2,1,0:T(8,128)} %get-tuple-element.8.hess_ref, f32[256,256]{1,0:T(8,128)} %get-tuple-element.9.inv_ref, bf16[1024,256]{1,0:T(8,128)(2,1)} %get-tuple-element.10.error_ref, bf16[1024,1792]{1,0:T(8,128)(2,1)} %weights_ref.1), custom_call_target="tpu_custom_call" | custom-call | tf_op jit(solution)/shard_map/update/pallas_call | solution.py:462
  (2 shorter events, 0.0 us)

commit v2 on v1

--- a/solution.py
+++ b/solution.py
@@ -10,6 +10,7 @@
 PANEL = 256
 QBLOCK = 128
 CHUNK = 256
+LAG = 4
 SQUARINGS = 18
 POLISH = 2
 MESH = pl.DeviceIdType.MESH
@@ -21,6 +22,14 @@
     return jnp.dot(left, right, precision=lax.Precision.HIGHEST, preferred_element_type=F32)
 
 
+def three(left, right):
+    l_top, l_low = split(left)
+    r_top, r_low = split(right)
+    return (jnp.dot(l_top, r_top, preferred_element_type=F32)
+            + jnp.dot(l_top, r_low, preferred_element_type=F32)
+            + jnp.dot(l_low, r_top, preferred_element_type=F32))
+
+
 def split(value):
     top = value.astype(BF16)
     return top, (value - top.astype(F32)).astype(BF16)
@@ -28,9 +37,9 @@
 
 def exchange_kernel(
     sizes,
-    panel_ref, error_ref, quant_ref, scale_ref,
-    hess_ref, inv_ref, error_out,
-    acts, quant, part, summed, diag_part, diag, square, inverse, scaled,
+    quant_ref, exps_hbm, weights_ref, keep_ref,
+    product_ref, error_out,
+    exps_ref, raw, acts, quant, weights, keep, hess_ref, part, summed, diag_part, diag, square, inverse, scaled,
     load_sem, quant_sem, arrive, send_z, send_y, send_c,
     diag_send, diag_recv, half_send, half_recv,
     err_send, err_recv,
@@ -76,7 +85,19 @@
         return pl.ds(pl.multiple_of(c * size, size), size)
 
     def load(c):
-        return pltpu.make_async_copy(panel_ref.at[rows_of(c)], acts.at[rows_of(c)], arrive.at[c])
+        return pltpu.make_async_copy(
+            quant_ref.at[rows_of(c), pl.ds(0, PANEL)], raw.at[rows_of(c)], arrive.at[c])
+
+    def error_load():
+        return (pltpu.make_async_copy(weights_ref.at[:, pl.ds(0, PANEL)], weights, load_sem.at[0]),
+                pltpu.make_async_copy(keep_ref, keep, load_sem.at[1]))
+
+    def scales_of(c):
+        exps = exps_ref[:, rows_of(c)].astype(F32)
+        return jnp.exp2(exps).T
+
+    def spread(column):
+        return jnp.broadcast_to(column, (CHUNK, QBLOCK)).astype(BF16)
 
     def send(c, target, sem):
         return pltpu.make_async_remote_copy(
@@ -88,11 +109,15 @@
         return pltpu.make_async_copy(
             quant_ref.at[rows_of(c), cols], quant.at[rows_of(c)], quant_sem.at[c])
 
+    exps_copy = pltpu.make_async_copy(exps_hbm, exps_ref, load_sem.at[2])
+    exps_copy.start()
+
     @pl.when(is_source)
     def _():
         for c in range(n_chunks):
             load(c).start()
-        pltpu.make_async_copy(error_ref, error_out, load_sem.at[0]).start()
+        for copy in error_load():
+            copy.start()
 
     for c in range(n_chunks):
         quant_load(c).start()
@@ -101,6 +126,7 @@
     for device in greeted:
         pl.semaphore_signal(barrier, inc=1, device_id=device, device_id_type=MESH)
     pl.semaphore_wait(barrier, len(greeted))
+    exps_copy.wait()
 
     def forward(c):
         @pl.when(can_z)
@@ -117,14 +143,27 @@
 
     @pl.when(is_source)
     def _():
+        def scale(c):
+            load(c).wait()
+            scales = scales_of(c)
+            for b in range(PANEL // QBLOCK):
+                cols = slice(b * QBLOCK, (b + 1) * QBLOCK)
+                acts[rows_of(c), cols] = raw[rows_of(c), cols] * spread(scales[:, b:b + 1])
+
+        def pass_on(j):
+            forward(own(j))
+            send(other(j), to_c, send_c).start()
+
         def body(j, carry):
-            load(own(j)).wait()
-            forward(own(j))
-            load(other(j)).wait()
-            send(other(j), to_c, send_c).start()
+            scale(own(j))
+            scale(other(j))
+            pass_on(j - 1)
             return carry
 
-        lax.fori_loop(0, n_pairs, body, 0)
+        scale(0)
+        scale(1)
+        lax.fori_loop(1, n_pairs, body, 0)
+        pass_on(n_pairs - 1)
 
         def gram(c, carry):
             block = acts[rows_of(c), :]
@@ -146,11 +185,12 @@
 
     def accumulate(c, first):
         quant_load(c).wait()
-        scales = scale_ref[rows_of(c), :]
+        scales = scales_of(c)
         blocks = []
-        for b in range(n_quant // QBLOCK):
-            scale = jnp.broadcast_to(scales[:, b:b + 1], (CHUNK, QBLOCK)).astype(BF16)
-            blocks.append(quant[rows_of(c), b * QBLOCK:(b + 1) * QBLOCK] * scale)
+        n_blocks = n_quant // QBLOCK
+        for b in range(n_blocks):
+            column = jnp.where(row == 0, scales[:, b:b + 1], scales[:, n_blocks + b:n_blocks + b + 1])
+            blocks.append(quant[rows_of(c), b * QBLOCK:(b + 1) * QBLOCK] * spread(column))
         value = jnp.concatenate(blocks, axis=1)
         term = lax.dot_general(
             acts[rows_of(c), :], value, (((0,), (0,)), ((), ())), preferred_element_type=F32)
@@ -161,7 +201,7 @@
             else:
                 part[i] += piece
 
-    def pair(j, first):
+    def own_step(j, first):
         @pl.when(jnp.logical_not(is_source))
         def _():
             send(own(j), to_c, send_c).wait_recv()
@@ -169,19 +209,30 @@
 
         accumulate(own(j), first)
 
+    def other_step(j):
         @pl.when(jnp.logical_not(is_source))
         def _():
             send(other(j), to_c, send_c).wait_recv()
 
         accumulate(other(j), False)
 
-    pair(0, True)
-
-    def later(j, carry):
-        pair(j, False)
+    def only_own(j, carry):
+        own_step(j, False)
         return carry
 
-    lax.fori_loop(1, n_pairs, later, 0)
+    def both(j, carry):
+        own_step(j, False)
+        other_step(j - LAG)
+        return carry
+
+    def only_other(j, carry):
+        other_step(j)
+        return carry
+
+    own_step(0, True)
+    lax.fori_loop(1, LAG, only_own, 0)
+    lax.fori_loop(LAG, n_pairs, both, 0)
+    lax.fori_loop(n_pairs - LAG, n_pairs, only_other, 0)
 
     def red_copy(i, k, device):
         dest = device[0]
@@ -234,6 +285,9 @@
 
     @pl.when(is_source)
     def _():
+        for copy in error_load():
+            copy.wait()
+        error_out[...] = jnp.where(keep[...] == 0, weights[...].astype(F32), 0.0).astype(BF16)
         for k, device in enumerate(peers):
             diag_copy(diag_part, diag_send, diag_recv, tok, k, device).wait_recv()
         total = diag_part[0]
@@ -242,47 +296,9 @@
         diag[...] = total
         half_forward()
         half_copy(1, to_c, 3).start()
-        pltpu.make_async_copy(error_ref, error_out, load_sem.at[0]).wait()
         for j in range(n_err // 2):
             err_forward(own(j))
             err_copy(other(j), to_c, 2).start()
-
-    @pl.when(jnp.logical_not(is_source))
-    def _():
-        half_copy(core, to_c, 0).wait_recv()
-        half_forward()
-        for j in range(n_err // 2):
-            err_copy(own(j), to_c, 0).wait_recv()
-            err_forward(own(j))
-        half_copy(1 - core, to_c, 0).wait_recv()
-
-    eye = (lax.broadcasted_iota(jnp.int32, (PANEL, PANEL), 0)
-           == lax.broadcasted_iota(jnp.int32, (PANEL, PANEL), 1)).astype(F32)
-    block = diag[...]
-    trace = jnp.sum(jnp.sum(block * eye, axis=1, keepdims=True), axis=0, keepdims=True)
-    damped = block + (0.01 / PANEL) * trace * eye
-    shrink = 1.0 / (1.01 * trace)
-    scaled[...] = damped * shrink
-    square[...] = eye - scaled[...]
-    inverse[...] = eye + square[...]
-
-    def double(s, carry):
-        r = square[...]
-        r2 = high(r, r)
-        square[...] = r2
-        x = inverse[...]
-        inverse[...] = x + high(x, r2)
-        return carry
-
-    lax.fori_loop(0, SQUARINGS, double, 0)
-
-    def polish(s, carry):
-        x = inverse[...]
-        inverse[...] = x + high(x, eye - high(scaled[...], x))
-        return carry
-
-    lax.fori_loop(0, POLISH, polish, 0)
-    inv_ref[...] = inverse[...] * shrink
 
     def all_copy(i, k, device):
         piece = hess_ref.at[row, i, rows_of(tok, strip)]
@@ -307,14 +323,65 @@
         for k, device in enumerate(peers):
             all_copy(i, k, device).start()
         row_copy(i, 0).start()
+
+    @pl.when(jnp.logical_not(is_source))
+    def _():
+        half_copy(core, to_c, 0).wait_recv()
+        half_forward()
+        for j in range(n_err // 2):
+            err_copy(own(j), to_c, 0).wait_recv()
+            err_forward(own(j))
+        half_copy(1 - core, to_c, 0).wait_recv()
+
+    eye = (lax.broadcasted_iota(jnp.int32, (PANEL, PANEL), 0)
+           == lax.broadcasted_iota(jnp.int32, (PANEL, PANEL), 1)).astype(F32)
+    block = diag[...]
+    trace = jnp.sum(jnp.sum(block * eye, axis=1, keepdims=True), axis=0, keepdims=True)
+    shrink = 1.0 / (1.01 * trace)
+    scaled[...] = (block + (0.01 / PANEL) * trace * eye) * shrink
+    square[...] = eye - scaled[...]
+    inverse[...] = eye + square[...]
+
+    def double(_, carry):
+        r = square[...]
+        r2 = three(r, r)
+        square[...] = r2
+        x = inverse[...]
+        inverse[...] = x + three(x, r2)
+        return carry
+
+    steps = -(-SQUARINGS // (n_feat - 1))
     for i in range(n_feat):
+        lax.fori_loop(0, steps if i else SQUARINGS - steps * (n_feat - 1), double, 0)
         for k, device in enumerate(peers):
             all_copy(i, n_tok - 2 - k, device).wait_recv()
             row_copy(i, k + 1).start()
 
+    def polish(_, carry):
+        x = inverse[...]
+        inverse[...] = x + high(eye - high(x, scaled[...]), x)
+        return carry
+
+    lax.fori_loop(0, POLISH, polish, 0)
+    top, low = split(inverse[...] * shrink)
+
+    def multiply(r, i):
+        h_top, h_low = split(hess_ref[r, i])
+        w_top, w_low = split(
+            jnp.dot(top, h_top, preferred_element_type=F32)
+            + jnp.dot(top, h_low, preferred_element_type=F32)
+            + jnp.dot(low, h_top, preferred_element_type=F32))
+        cols = pl.ds(pl.multiple_of((r * n_feat + i) * width, width), width)
+        product_ref[:PANEL, cols] = w_top
+        product_ref[PANEL:, cols] = w_low
+
+    for i in range(n_feat):
+        multiply(row, i)
     for i in range(n_feat):
         for k in range(n_tok):
             row_copy(i, k).wait_recv()
+        multiply(1 - row, i)
+
     for i in range(n_feat):
         for k, device in enumerate(peers):
             red_copy(i, k, device).wait_send()
@@ -384,31 +451,36 @@
         recv_sem=recv_sem.at[n - 2 - k], device_id=device, device_id_type=MESH)
 
 
-def exchange(panel, error, quantized, scales):
+def exchange(quantized, exponents, weights, keep_mask):
     tokens, columns = quantized.shape
+    rows = weights.shape[0]
     n_tok = lax.axis_size("tok")
     n_quant = columns // lax.axis_size("row")
     width = 128
     n_feat = n_quant // width
     n_chunks = tokens // CHUNK
-    n_err = error.shape[0] // CHUNK
+    n_err = rows // CHUNK
     strip = PANEL // n_tok
     sizes = (n_chunks, n_chunks // 2, n_err, width, n_feat, n_tok)
     dma = pltpu.SemaphoreType.DMA
     vmem = pl.BlockSpec(memory_space=pltpu.VMEM)
-    hbm = pl.BlockSpec(memory_space=pl.ANY)
+    hbm = pl.BlockSpec(memory_space=pltpu.HBM)
     return pl.pallas_call(
         functools.partial(exchange_kernel, sizes),
         out_shape=(
-            jax.ShapeDtypeStruct((2, n_feat, PANEL, width), F32),
-            jax.ShapeDtypeStruct((PANEL, PANEL), F32),
-            jax.ShapeDtypeStruct(error.shape, BF16),
+            jax.ShapeDtypeStruct((2 * PANEL, columns), BF16),
+            jax.ShapeDtypeStruct((rows, PANEL), BF16),
         ),
-        in_specs=[hbm, hbm, hbm, vmem],
-        out_specs=(vmem, vmem, vmem),
+        in_specs=[hbm, hbm, hbm, hbm],
+        out_specs=(vmem, vmem),
         scratch_shapes=[
+            pltpu.VMEM(exponents.T.shape, jnp.int32),
+            pltpu.VMEM((tokens, PANEL), BF16),
             pltpu.VMEM((tokens, PANEL), BF16),
             pltpu.VMEM((tokens, n_quant), BF16),
+            pltpu.VMEM((rows, PANEL), BF16),
+            pltpu.VMEM((rows, PANEL), jnp.int32),
+            pltpu.VMEM((2, n_feat, PANEL, width), F32),
             pltpu.VMEM((n_feat, PANEL, width), F32),
             pltpu.VMEM((n_feat, n_tok, strip, width), F32),
             pltpu.VMEM((n_tok, PANEL, PANEL), F32),
@@ -416,7 +488,7 @@
             pltpu.VMEM((PANEL, PANEL), F32),
             pltpu.VMEM((PANEL, PANEL), F32),
             pltpu.VMEM((PANEL, PANEL), F32),
-            dma((1,)), dma((n_chunks,)), dma((n_chunks,)),
+            dma((3,)), dma((n_chunks,)), dma((n_chunks,)),
             dma((n_chunks,)), dma((n_chunks,)), dma((n_chunks,)),
             dma((n_tok - 1,)), dma((n_tok - 1,)), dma((4,)), dma((2,)),
             dma((3, n_err)), dma((n_err,)),
@@ -425,31 +497,16 @@
             dma((n_feat, n_tok)), dma((n_feat, n_tok)),
         ],
         compiler_params=pltpu.CompilerParams(
-            collective_id=0, has_side_effects=True, vmem_limit_bytes=60 * 1024 * 1024),
+            collective_id=0, has_side_effects=True, vmem_limit_bytes=32 * 1024 * 1024),
         name="exchange",
-    )(panel, error, quantized, scales)
-
-
-def update_kernel(feat_ref, hess_ref, inv_ref, error_ref, weights_ref, out_ref, product):
-    n_rows, n_feat, _, width = hess_ref.shape
-
-    @pl.when(pl.program_id(0) == 0)
-    def _():
-        top, low = split(inv_ref[...])
-        for r in range(n_rows):
-            for i in range(n_feat):
-                h_top, h_low = split(hess_ref[r, i])
-                value = (jnp.dot(top, h_top, preferred_element_type=F32)
-                         + jnp.dot(top, h_low, preferred_element_type=F32)
-                         + jnp.dot(low, h_top, preferred_element_type=F32))
-                w_top, w_low = split(value)
-                cols = pl.ds((r * n_feat + i) * width, width)
-                product[:PANEL, cols] = w_top
-                product[PANEL:, cols] = w_low
-
+    )(*[pltpu.with_memory_space_constraint(x, pltpu.HBM)
+        for x in (quantized, exponents.T, weights, keep_mask)])
+
+
+def update_kernel(feat_ref, product_ref, error_ref, weights_ref, out_ref):
     error = error_ref[...]
     both = jnp.concatenate([error, error], axis=1)
-    update = jnp.dot(both, product[...], preferred_element_type=F32)
+    update = jnp.dot(both, product_ref[...], preferred_element_type=F32)
     out_ref[...] = (weights_ref[...].astype(F32) + update).astype(BF16)
 
     @pl.when(feat_ref[0] == 0)
@@ -457,7 +514,7 @@
         out_ref[:, :PANEL] = weights_ref[:, :PANEL] - error
 
 
-def apply_update(feat, hess, inv, error, weights, tile=128):
+def apply_update(feat, product, error, weights, tile=128):
     rows, columns = weights.shape
     return pl.pallas_call(
         update_kernel,
@@ -466,31 +523,19 @@
         in_specs=[
             pl.BlockSpec(memory_space=pltpu.SMEM),
             pl.BlockSpec(memory_space=pltpu.VMEM),
-            pl.BlockSpec(memory_space=pltpu.VMEM),
             pl.BlockSpec((tile, PANEL), lambda g: (g, 0)),
             pl.BlockSpec((tile, columns), lambda g: (g, 0)),
         ],
         out_specs=pl.BlockSpec((tile, columns), lambda g: (g, 0)),
-        scratch_shapes=[pltpu.VMEM((2 * PANEL, columns), BF16)],
+        compiler_params=pltpu.CompilerParams(vmem_limit_bytes=24 * 1024 * 1024),
         name="update",
-    )(feat, hess, inv, error, weights)
+    )(feat, product, error, weights)
 
 
 def shards(quantized, exponents, weights, keep_mask):
-    tokens = quantized.shape[0]
-    blocks = exponents.shape[1]
-    scales = jnp.exp2(exponents.astype(F32))
-    own = PANEL // QBLOCK
-    panel = (
-        quantized[:, :PANEL].reshape(tokens, own, QBLOCK)
-        * scales[:, :own].astype(BF16)[:, :, None]
-    ).reshape(tokens, PANEL)
-    half = blocks // lax.axis_size("row")
-    row_scales = lax.dynamic_slice_in_dim(scales, lax.axis_index("row") * half, half, 1)
-    error = jnp.where(keep_mask == 0, weights[:, :PANEL], jnp.zeros((), BF16))
-    hess, inv, error = exchange(panel, error, quantized, row_scales)
+    product, error = exchange(quantized, exponents, weights, keep_mask)
     feat = lax.axis_index("feat").astype(jnp.int32).reshape(1)
-    return apply_update(feat, hess, inv, error, weights)
+    return apply_update(feat, product, error, weights)
 
 
 def solution(mesh):

time: 171 us -> 83.4 us (0.49)
  Pallas kernels: 149 us -> 83.3 us
  local copies, waits for them, and re-layouts: 14.2 us -> 0.01 us
  other arithmetic: 6.46 us -> 0 us
    pallas_call x1, Pallas kernels: 139 us -> 78.1 us  [exchange(): pl.pallas_call(functools.partial(exchange_kernel, sizes), out_shape=(jax....]
    mul x1 -> x0, local copies, waits for them, and re-layouts: 11.6 us -> none  [shards(): quantized[:, :PANEL].reshape(tokens, own, QBLOCK)]
    pallas_call x1, Pallas kernels: 10.1 us -> 5.17 us  [apply_update(): pl.pallas_call(update_kernel, grid=(rows // tile,), out_shape=jax.ShapeDt...]
    mul x1 -> x0, other arithmetic: 3.18 us -> none  [shards(): quantized[:, :PANEL].reshape(tokens, own, QBLOCK)]
    select_n x1 -> x0, other arithmetic: 2.28 us -> none  [shards(): error = jnp.where(keep_mask == 0, weights[:, :PANEL], jnp.zeros((), BF16))]
    unnamed x1 -> x2, local copies, waits for them, and re-layouts: 1.99 us -> 0.01 us
where the time goes in v2:
time: 83.4 us; the launch traced here: 83.3 us
  Pallas kernels  83.3 us (100%)
    pallas_call x1, Pallas kernels, exchange(): pl.pallas_call(functools.partial(exchange_kernel, sizes), out_shape=(jax....  78.1 us
    pallas_call x1, Pallas kernels, apply_update(): pl.pallas_call(update_kernel, grid=(rows // tile,), out_shape=jax.ShapeDt...  5.17 us

profile of v2, /device:TPU:104, one launch (start us, length us, event | category | flops | bytes accessed | tf_op | source)
XLA Modules:
  0.0 83.3 jit_solution(12711691268465140026)
XLA Ops:
  0.0 0.0 copy-start
  0.0 78.1 %exchange.1 = (bf16[512,1792]{1,0:T(8,128)(2,1)S(1)}, bf16[1024,256]{1,0:T(8,128)(2,1)S(1)}) custom-call(bf16[4096,1792]{1,0:T(8,128)(2,1)} %quant_ref.1, s32[14,4096]{1,0:T(8,128)} %bitcast.2, bf16[1024,1792]{1,0:T(8,128)(2,1)} %weights_ref.3, s32[1024,256]{1,0:T(8,128)} %keep_ref.1), custom_call_target="tpu_custom_call" | custom-call | tf_op jit(solution)/shard_map/exchange/pallas_call | solution.py:468
  78.2 0.0 copy-done
  78.2 5.2 %update.1 = bf16[1024,1792]{1,0:T(8,128)(2,1)} custom-call(s32[1]{0:T(128)} %bitcast.feat_ref, bf16[512,1792]{1,0:T(8,128)(2,1)S(1)} %get-tuple-element.7.product_ref, bf16[1024,256]{1,0:T(8,128)(2,1)S(1)} %get-tuple-element.8.error_ref, bf16[1024,1792]{1,0:T(8,128)(2,1)S(1)} %copy-done), custom_call_target="tpu_custom_call" | custom-call | tf_op jit(solution)/shard_map/update/pallas_call | solution.py:519
Async XLA Ops:
  0.0 78.2 %copy-start = (bf16[1024,1792]{1,0:T(8,128)(2,1)S(1)}, bf16[1024,1792]{1,0:T(8,128)(2,1)}, u32[]{:S(2)}) copy-start(bf16[1024,1792]{1,0:T(8,128)(2,1)} %weights_ref.3) | copy-start | bytes 11010052

commit v3 on v2

--- a/solution.py
+++ b/solution.py
@@ -10,7 +10,7 @@
 PANEL = 256
 QBLOCK = 128
 CHUNK = 256
-LAG = 4
+LAG = 6
 SQUARINGS = 18
 POLISH = 2
 MESH = pl.DeviceIdType.MESH
@@ -74,6 +74,8 @@
     is_twin = feat == 1
     can_z = jnp.logical_and(even_y, hops < 3)
     not_twin = feat != 1
+    chain_z = hops < 3
+    root_y = jnp.logical_and(even_y, z == 0)
 
     def own(j):
         return 2 * j + core
@@ -258,11 +260,11 @@
             device_id=target, device_id_type=MESH)
 
     def half_forward():
-        @pl.when(can_z)
+        @pl.when(chain_z)
         def _():
             half_copy(core, to_z, 0).start()
 
-        @pl.when(even_y)
+        @pl.when(root_y)
         def _():
             half_copy(core, to_y, 1).start()
 
@@ -271,11 +273,11 @@
             half_copy(core, to_c, 2).start()
 
     def err_forward(c):
-        @pl.when(can_z)
+        @pl.when(chain_z)
         def _():
             err_copy(c, to_z, 0).start()
 
-        @pl.when(even_y)
+        @pl.when(root_y)
         def _():
             err_copy(c, to_y_same, 1).start()
 
@@ -300,6 +302,12 @@
             err_forward(own(j))
             err_copy(other(j), to_c, 2).start()
 
+    @pl.when(jnp.logical_not(is_source))
+    def _():
+        half_copy(core, to_c, 0).wait_recv()
+        half_forward()
+        half_copy(1 - core, to_c, 0).wait_recv()
+
     def all_copy(i, k, device):
         piece = hess_ref.at[row, i, rows_of(tok, strip)]
         return pltpu.make_async_remote_copy(
@@ -326,12 +334,9 @@
 
     @pl.when(jnp.logical_not(is_source))
     def _():
-        half_copy(core, to_c, 0).wait_recv()
-        half_forward()
         for j in range(n_err // 2):
             err_copy(own(j), to_c, 0).wait_recv()
             err_forward(own(j))
-        half_copy(1 - core, to_c, 0).wait_recv()
 
     eye = (lax.broadcasted_iota(jnp.int32, (PANEL, PANEL), 0)
            == lax.broadcasted_iota(jnp.int32, (PANEL, PANEL), 1)).astype(F32)
@@ -417,13 +422,13 @@
 
     lax.fori_loop(0, n_pairs, drain, 0)
 
-    @pl.when(can_z)
+    @pl.when(chain_z)
     def _():
         half_copy(core, to_z, 0).wait_send()
         for j in range(n_err // 2):
             err_copy(own(j), to_z, 0).wait_send()
 
-    @pl.when(even_y)
+    @pl.when(root_y)
     def _():
         half_copy(core, to_y, 1).wait_send()
         for j in range(n_err // 2):
@@ -514,7 +519,7 @@
         out_ref[:, :PANEL] = weights_ref[:, :PANEL] - error
 
 
-def apply_update(feat, product, error, weights, tile=128):
+def apply_update(feat, product, error, weights, tile=512):
     rows, columns = weights.shape
     return pl.pallas_call(
         update_kernel,

time: 83.4 us -> 74.2 us (0.89)
  Pallas kernels: 83.3 us -> 74 us
    pallas_call x1, Pallas kernels: 78.1 us -> 70.5 us  [exchange(): pl.pallas_call(functools.partial(exchange_kernel, sizes), out_shape=(jax....]
    pallas_call x1, Pallas kernels: 5.17 us -> 3.52 us  [apply_update(): pl.pallas_call(update_kernel, grid=(rows // tile,), out_shape=jax.ShapeDt...]
where the time goes in v3:
time: 74.2 us; the launch traced here: 74 us
  Pallas kernels  74 us (100%)
    pallas_call x1, Pallas kernels, exchange(): pl.pallas_call(functools.partial(exchange_kernel, sizes), out_shape=(jax....  70.5 us
    pallas_call x1, Pallas kernels, apply_update(): pl.pallas_call(update_kernel, grid=(rows // tile,), out_shape=jax.ShapeDt...  3.52 us

profile of v3, /device:TPU:104, one launch (start us, length us, event | category | flops | bytes accessed | tf_op | source)
XLA Modules:
  0.0 74.0 jit_solution(269355360098940053)
XLA Ops:
  0.0 0.0 copy-start
  0.0 70.5 %exchange.1 = (bf16[512,1792]{1,0:T(8,128)(2,1)S(1)}, bf16[1024,256]{1,0:T(8,128)(2,1)S(1)}) custom-call(bf16[4096,1792]{1,0:T(8,128)(2,1)} %quant_ref.1, s32[14,4096]{1,0:T(8,128)} %bitcast.2, bf16[1024,1792]{1,0:T(8,128)(2,1)} %weights_ref.3, s32[1024,256]{1,0:T(8,128)} %keep_ref.1), custom_call_target="tpu_custom_call" | custom-call | tf_op jit(solution)/shard_map/exchange/pallas_call | solution.py:473
  70.5 0.0 copy-done
  70.5 3.5 %update.1 = bf16[1024,1792]{1,0:T(8,128)(2,1)} custom-call(s32[1]{0:T(128)} %bitcast.feat_ref, bf16[512,1792]{1,0:T(8,128)(2,1)S(1)} %get-tuple-element.7.product_ref, bf16[1024,256]{1,0:T(8,128)(2,1)S(1)} %get-tuple-element.8.error_ref, bf16[1024,1792]{1,0:T(8,128)(2,1)S(1)} %copy-done), custom_call_target="tpu_custom_call" | custom-call | tf_op jit(solution)/shard_map/update/pallas_call | solution.py:524
Async XLA Ops:
  0.0 70.5 %copy-start = (bf16[1024,1792]{1,0:T(8,128)(2,1)S(1)}, bf16[1024,1792]{1,0:T(8,128)(2,1)}, u32[]{:S(2)}) copy-start(bf16[1024,1792]{1,0:T(8,128)(2,1)} %weights_ref.3) | copy-start | bytes 11010052

commit v4 on v2

--- a/solution.py
+++ b/solution.py
@@ -10,7 +10,8 @@
 PANEL = 256
 QBLOCK = 128
 CHUNK = 256
-LAG = 4
+PIECE = 128
+LAG = 8
 SQUARINGS = 18
 POLISH = 2
 MESH = pl.DeviceIdType.MESH
@@ -72,8 +73,9 @@
     even_y = y_lo == 0
     is_source = feat == 0
     is_twin = feat == 1
-    can_z = jnp.logical_and(even_y, hops < 3)
     not_twin = feat != 1
+    chain_z = hops < 3
+    root_y = jnp.logical_and(even_y, z == 0)
 
     def own(j):
         return 2 * j + core
@@ -99,10 +101,17 @@
     def spread(column):
         return jnp.broadcast_to(column, (CHUNK, QBLOCK)).astype(BF16)
 
-    def send(c, target, sem):
+    def hub(j):
+        return 2 * own(j) + y_lo
+
+    def leaf(j):
+        return 2 * own(j) + 1 - y_lo
+
+    def send(p, target, sem):
+        piece = acts.at[rows_of(p, PIECE)]
         return pltpu.make_async_remote_copy(
-            src_ref=acts.at[rows_of(c)], dst_ref=acts.at[rows_of(c)], send_sem=sem.at[c],
-            recv_sem=arrive.at[c], device_id=target, device_id_type=MESH)
+            src_ref=piece, dst_ref=piece, send_sem=sem.at[p], recv_sem=arrive.at[p],
+            device_id=target, device_id_type=MESH)
 
     def quant_load(c):
         cols = pl.ds(pl.multiple_of(row * n_quant, 128), n_quant)
@@ -128,18 +137,69 @@
     pl.semaphore_wait(barrier, len(greeted))
     exps_copy.wait()
 
-    def forward(c):
-        @pl.when(can_z)
-        def _():
-            send(c, to_z, send_z).start()
-
-        @pl.when(even_y)
-        def _():
-            send(c, to_y, send_y).start()
+    def hub_forward(j):
+        @pl.when(chain_z)
+        def _():
+            send(hub(j), to_z, send_z).start()
+
+        @pl.when(z != 0)
+        def _():
+            send(hub(j), to_y, send_y).start()
 
         @pl.when(not_twin)
         def _():
-            send(c, to_c, send_c).start()
+            send(hub(j), to_c, send_c).start()
+
+    def leaf_forward(j):
+        @pl.when(root_y)
+        def _():
+            send(leaf(j), to_y, send_y).start()
+
+        @pl.when(not_twin)
+        def _():
+            send(leaf(j), to_c, send_c).start()
+
+    def late_forward(j, carry):
+        send(hub(j), to_y, send_y).start()
+        return carry
+
+    def half_copy(h, target, slot):
+        return pltpu.make_async_remote_copy(
+            src_ref=diag.at[rows_of(h, PANEL // 2)], dst_ref=diag.at[rows_of(h, PANEL // 2)],
+            send_sem=half_send.at[slot], recv_sem=half_recv.at[h],
+            device_id=target, device_id_type=MESH)
+
+    def err_copy(c, target, slot):
+        return pltpu.make_async_remote_copy(
+            src_ref=error_out.at[rows_of(c)], dst_ref=error_out.at[rows_of(c)],
+            send_sem=err_send.at[slot, c], recv_sem=err_recv.at[c],
+            device_id=target, device_id_type=MESH)
+
+    def half_forward():
+        @pl.when(chain_z)
+        def _():
+            half_copy(core, to_z, 0).start()
+
+        @pl.when(root_y)
+        def _():
+            half_copy(core, to_y, 1).start()
+
+        @pl.when(not_twin)
+        def _():
+            half_copy(core, to_c, 2).start()
+
+    def err_forward(c):
+        @pl.when(chain_z)
+        def _():
+            err_copy(c, to_z, 0).start()
+
+        @pl.when(root_y)
+        def _():
+            err_copy(c, to_y_same, 1).start()
+
+        @pl.when(not_twin)
+        def _():
+            err_copy(c, to_c, 2).start()
 
     @pl.when(is_source)
     def _():
@@ -151,8 +211,10 @@
                 acts[rows_of(c), cols] = raw[rows_of(c), cols] * spread(scales[:, b:b + 1])
 
         def pass_on(j):
-            forward(own(j))
-            send(other(j), to_c, send_c).start()
+            hub_forward(j)
+            leaf_forward(j)
+            for half in range(2):
+                send(2 * other(j) + half, to_c, send_c).start()
 
         def body(j, carry):
             scale(own(j))
@@ -164,6 +226,7 @@
         scale(1)
         lax.fori_loop(1, n_pairs, body, 0)
         pass_on(n_pairs - 1)
+        lax.fori_loop(0, n_pairs, late_forward, 0)
 
         def gram(c, carry):
             block = acts[rows_of(c), :]
@@ -183,56 +246,98 @@
         for k, device in enumerate(peers):
             diag_copy(diag_part, diag_send, diag_recv, tok, k, device).start()
 
-    def accumulate(c, first):
+    def prescale(c):
         quant_load(c).wait()
         scales = scales_of(c)
-        blocks = []
         n_blocks = n_quant // QBLOCK
         for b in range(n_blocks):
+            cols = slice(b * QBLOCK, (b + 1) * QBLOCK)
             column = jnp.where(row == 0, scales[:, b:b + 1], scales[:, n_blocks + b:n_blocks + b + 1])
-            blocks.append(quant[rows_of(c), b * QBLOCK:(b + 1) * QBLOCK] * spread(column))
-        value = jnp.concatenate(blocks, axis=1)
+            quant[rows_of(c), cols] = quant[rows_of(c), cols] * spread(column)
+
+    def accumulate(c):
         term = lax.dot_general(
-            acts[rows_of(c), :], value, (((0,), (0,)), ((), ())), preferred_element_type=F32)
+            acts[rows_of(c), :], quant[rows_of(c), :], (((0,), (0,)), ((), ())),
+            preferred_element_type=F32)
         for i in range(n_feat):
-            piece = term[:, i * width:(i + 1) * width]
-            if first:
-                part[i] = piece
-            else:
-                part[i] += piece
-
-    def own_step(j, first):
+            part[i] += term[:, i * width:(i + 1) * width]
+
+    def own_gram(j):
+        @pl.when(feat > 1)
+        def _():
+            send(leaf(j), to_c, send_c).wait_recv()
+            leaf_forward(j)
+
+        accumulate(own(j))
+
+    part[...] = jnp.zeros_like(part)
+
+    def hub_step(j, carry):
         @pl.when(jnp.logical_not(is_source))
         def _():
-            send(own(j), to_c, send_c).wait_recv()
-            forward(own(j))
-
-        accumulate(own(j), first)
-
-    def other_step(j):
+            send(hub(j), to_c, send_c).wait_recv()
+            hub_forward(j)
+
+        @pl.when(is_twin)
+        def _():
+            send(leaf(j), to_c, send_c).wait_recv()
+            leaf_forward(j)
+
+        @pl.when(jnp.logical_and(j >= LAG, feat > 1))
+        def _():
+            own_gram(j - LAG)
+
+        return carry
+
+    def prescale_step(c, carry):
+        prescale(c)
+        return carry
+
+    lax.fori_loop(0, jnp.where(feat > 1, n_chunks, 0), prescale_step, 0)
+    lax.fori_loop(0, n_pairs, hub_step, 0)
+
+    @pl.when(is_twin)
+    def _():
+        lax.fori_loop(0, n_pairs, late_forward, 0)
+
+    lax.fori_loop(jnp.where(feat > 1, n_chunks, 0), n_chunks, prescale_step, 0)
+
+    def own_step(j, carry):
+        own_gram(j)
+        return carry
+
+    @pl.when(is_source)
+    def _():
+        for k, device in enumerate(peers):
+            diag_copy(diag_part, diag_send, diag_recv, tok, k, device).wait_recv()
+        total = diag_part[0]
+        for t in range(1, n_tok):
+            total = total + diag_part[t]
+        diag[...] = total
+        for copy in error_load():
+            copy.wait()
+        error_out[...] = jnp.where(keep[...] == 0, weights[...].astype(F32), 0.0).astype(BF16)
+        half_forward()
+        half_copy(1, to_c, 3).start()
+
+    lax.fori_loop(jnp.where(feat > 1, n_pairs - LAG, 0), n_pairs, own_step, 0)
+
+    def other_step(j, carry):
         @pl.when(jnp.logical_not(is_source))
         def _():
-            send(other(j), to_c, send_c).wait_recv()
-
-        accumulate(other(j), False)
-
-    def only_own(j, carry):
-        own_step(j, False)
-        return carry
-
-    def both(j, carry):
-        own_step(j, False)
-        other_step(j - LAG)
-        return carry
-
-    def only_other(j, carry):
-        other_step(j)
-        return carry
-
-    own_step(0, True)
-    lax.fori_loop(1, LAG, only_own, 0)
-    lax.fori_loop(LAG, n_pairs, both, 0)
-    lax.fori_loop(n_pairs - LAG, n_pairs, only_other, 0)
+            for half in range(2):
+                send(2 * other(j) + half, to_c, send_c).wait_recv()
+
+        accumulate(other(j))
+        return carry
+
+    lax.fori_loop(0, n_pairs, other_step, 0)
+
+    @pl.when(is_source)
+    def _():
+        for j in range(n_err // 2):
+            err_forward(own(j))
+            err_copy(other(j), to_c, 2).start()
 
     def red_copy(i, k, device):
         dest = device[0]
@@ -245,60 +350,11 @@
         for k, device in enumerate(peers):
             red_copy(i, k, device).start()
 
-    def half_copy(h, target, slot):
-        return pltpu.make_async_remote_copy(
-            src_ref=diag.at[rows_of(h, PANEL // 2)], dst_ref=diag.at[rows_of(h, PANEL // 2)],
-            send_sem=half_send.at[slot], recv_sem=half_recv.at[h],
-            device_id=target, device_id_type=MESH)
-
-    def err_copy(c, target, slot):
-        return pltpu.make_async_remote_copy(
-            src_ref=error_out.at[rows_of(c)], dst_ref=error_out.at[rows_of(c)],
-            send_sem=err_send.at[slot, c], recv_sem=err_recv.at[c],
-            device_id=target, device_id_type=MESH)
-
-    def half_forward():
-        @pl.when(can_z)
-        def _():
-            half_copy(core, to_z, 0).start()
-
-        @pl.when(even_y)
-        def _():
-            half_copy(core, to_y, 1).start()
-
-        @pl.when(not_twin)
-        def _():
-            half_copy(core, to_c, 2).start()
-
-    def err_forward(c):
-        @pl.when(can_z)
-        def _():
-            err_copy(c, to_z, 0).start()
-
-        @pl.when(even_y)
-        def _():
-            err_copy(c, to_y_same, 1).start()
-
-        @pl.when(not_twin)
-        def _():
-            err_copy(c, to_c, 2).start()
-
-    @pl.when(is_source)
-    def _():
-        for copy in error_load():
-            copy.wait()
-        error_out[...] = jnp.where(keep[...] == 0, weights[...].astype(F32), 0.0).astype(BF16)
-        for k, device in enumerate(peers):
-            diag_copy(diag_part, diag_send, diag_recv, tok, k, device).wait_recv()
-        total = diag_part[0]
-        for t in range(1, n_tok):
-            total = total + diag_part[t]
-        diag[...] = total
+    @pl.when(jnp.logical_not(is_source))
+    def _():
+        half_copy(core, to_c, 0).wait_recv()
         half_forward()
-        half_copy(1, to_c, 3).start()
-        for j in range(n_err // 2):
-            err_forward(own(j))
-            err_copy(other(j), to_c, 2).start()
+        half_copy(1 - core, to_c, 0).wait_recv()
 
     def all_copy(i, k, device):
         piece = hess_ref.at[row, i, rows_of(tok, strip)]
@@ -324,14 +380,14 @@
             all_copy(i, k, device).start()
         row_copy(i, 0).start()
 
-    @pl.when(jnp.logical_not(is_source))
-    def _():
-        half_copy(core, to_c, 0).wait_recv()
-        half_forward()
-        for j in range(n_err // 2):
-            err_copy(own(j), to_c, 0).wait_recv()
-            err_forward(own(j))
-        half_copy(1 - core, to_c, 0).wait_recv()
+    def err_pass(ready):
+        @pl.when(jnp.logical_and(ready, jnp.logical_not(is_source)))
+        def _():
+            for j in range(n_err // 2):
+                err_copy(own(j), to_c, 0).wait_recv()
+                err_forward(own(j))
+
+    err_pass(hops <= 1)
 
     eye = (lax.broadcasted_iota(jnp.int32, (PANEL, PANEL), 0)
            == lax.broadcasted_iota(jnp.int32, (PANEL, PANEL), 1)).astype(F32)
@@ -353,6 +409,10 @@
     steps = -(-SQUARINGS // (n_feat - 1))
     for i in range(n_feat):
         lax.fori_loop(0, steps if i else SQUARINGS - steps * (n_feat - 1), double, 0)
+        if i == 2:
+            err_pass(hops == 2)
+        if i == 5:
+            err_pass(hops == 3)
         for k, device in enumerate(peers):
             all_copy(i, n_tok - 2 - k, device).wait_recv()
             row_copy(i, k + 1).start()
@@ -395,35 +455,39 @@
             err_copy(other(j), to_c, 0).wait_recv()
 
     def drain(j, carry):
-        c = own(j)
-
-        @pl.when(can_z)
-        def _():
-            send(c, to_z, send_z).wait_send()
-
-        @pl.when(even_y)
-        def _():
-            send(c, to_y, send_y).wait_send()
+        @pl.when(chain_z)
+        def _():
+            send(hub(j), to_z, send_z).wait_send()
+
+        @pl.when(jnp.logical_or(even_y, z != 0))
+        def _():
+            send(hub(j), to_y, send_y).wait_send()
+
+        @pl.when(root_y)
+        def _():
+            send(leaf(j), to_y, send_y).wait_send()
 
         @pl.when(not_twin)
         def _():
-            send(c, to_c, send_c).wait_send()
+            send(hub(j), to_c, send_c).wait_send()
+            send(leaf(j), to_c, send_c).wait_send()
 
         @pl.when(is_source)
         def _():
-            send(other(j), to_c, send_c).wait_send()
+            for half in range(2):
+                send(2 * other(j) + half, to_c, send_c).wait_send()
 
         return carry
 
     lax.fori_loop(0, n_pairs, drain, 0)
 
-    @pl.when(can_z)
+    @pl.when(chain_z)
     def _():
         half_copy(core, to_z, 0).wait_send()
         for j in range(n_err // 2):
             err_copy(own(j), to_z, 0).wait_send()
 
-    @pl.when(even_y)
+    @pl.when(root_y)
     def _():
         half_copy(core, to_y, 1).wait_send()
         for j in range(n_err // 2):
@@ -459,6 +523,7 @@
     width = 128
     n_feat = n_quant // width
     n_chunks = tokens // CHUNK
+    n_pieces = tokens // PIECE
     n_err = rows // CHUNK
     strip = PANEL // n_tok
     sizes = (n_chunks, n_chunks // 2, n_err, width, n_feat, n_tok)
@@ -488,8 +553,8 @@
             pltpu.VMEM((PANEL, PANEL), F32),
             pltpu.VMEM((PANEL, PANEL), F32),
             pltpu.VMEM((PANEL, PANEL), F32),
-            dma((3,)), dma((n_chunks,)), dma((n_chunks,)),
-            dma((n_chunks,)), dma((n_chunks,)), dma((n_chunks,)),
+            dma((3,)), dma((n_chunks,)), dma((n_pieces,)),
+            dma((n_pieces,)), dma((n_pieces,)), dma((n_pieces,)),
             dma((n_tok - 1,)), dma((n_tok - 1,)), dma((4,)), dma((2,)),
             dma((3, n_err)), dma((n_err,)),
             dma((n_feat, n_tok - 1)), dma((n_feat, n_tok - 1)),
@@ -514,7 +579,7 @@
         out_ref[:, :PANEL] = weights_ref[:, :PANEL] - error
 
 
-def apply_update(feat, product, error, weights, tile=128):
+def apply_update(feat, product, error, weights, tile=512):
     rows, columns = weights.shape
     return pl.pallas_call(
         update_kernel,

time: 83.4 us -> 70 us (0.84)
  the two profiles are of different devices: /device:TPU:104 before, /device:TPU:96 now
where the time goes in v4:
time: 70 us; the launch traced here: 69.9 us
  Pallas kernels  69.8 us (100%)
    pallas_call x1, Pallas kernels, exchange(): pl.pallas_call(functools.partial(exchange_kernel, sizes), out_shape=(jax....  66.3 us
    pallas_call x1, Pallas kernels, apply_update(): pl.pallas_call(update_kernel, grid=(rows // tile,), out_shape=jax.ShapeDt...  3.52 us

profile of v4, /device:TPU:96, one launch (start us, length us, event | category | flops | bytes accessed | tf_op | source)
XLA Modules:
  0.0 69.9 jit_solution(9805496641332237052)
XLA Ops:
  0.0 0.0 copy-start
  0.0 66.3 %exchange.1 = (bf16[512,1792]{1,0:T(8,128)(2,1)S(1)}, bf16[1024,256]{1,0:T(8,128)(2,1)S(1)}) custom-call(bf16[4096,1792]{1,0:T(8,128)(2,1)} %quant_ref.1, s32[14,4096]{1,0:T(8,128)} %bitcast.2, bf16[1024,1792]{1,0:T(8,128)(2,1)} %weights_ref.3, s32[1024,256]{1,0:T(8,128)} %keep_ref.1), custom_call_target="tpu_custom_call" | custom-call | tf_op jit(solution)/shard_map/exchange/pallas_call | solution.py:533
  66.3 0.0 copy-done
  66.3 3.5 %update.1 = bf16[1024,1792]{1,0:T(8,128)(2,1)} custom-call(s32[1]{0:T(128)} %bitcast.feat_ref, bf16[512,1792]{1,0:T(8,128)(2,1)S(1)} %get-tuple-element.7.product_ref, bf16[1024,256]{1,0:T(8,128)(2,1)S(1)} %get-tuple-element.8.error_ref, bf16[1024,1792]{1,0:T(8,128)(2,1)S(1)} %copy-done), custom_call_target="tpu_custom_call" | custom-call | tf_op jit(solution)/shard_map/update/pallas_call | solution.py:584
Async XLA Ops:
  0.0 66.3 %copy-start = (bf16[1024,1792]{1,0:T(8,128)(2,1)S(1)}, bf16[1024,1792]{1,0:T(8,128)(2,1)}, u32[]{:S(2)}) copy-start(bf16[1024,1792]{1,0:T(8,128)(2,1)} %weights_ref.3) | copy-start | bytes 11010052

commit v5 on v4

--- a/solution.py
+++ b/solution.py
@@ -11,7 +11,7 @@
 QBLOCK = 128
 CHUNK = 256
 PIECE = 128
-LAG = 8
+LAG = 5
 SQUARINGS = 18
 POLISH = 2
 MESH = pl.DeviceIdType.MESH
@@ -409,9 +409,9 @@
     steps = -(-SQUARINGS // (n_feat - 1))
     for i in range(n_feat):
         lax.fori_loop(0, steps if i else SQUARINGS - steps * (n_feat - 1), double, 0)
-        if i == 2:
+        if i == 3:
             err_pass(hops == 2)
-        if i == 5:
+        if i == 6:
             err_pass(hops == 3)
         for k, device in enumerate(peers):
             all_copy(i, n_tok - 2 - k, device).wait_recv()

time: 70 us -> 70 us (level)
  no operation moved by 1% of the time
where the time goes in v5:
time: 70 us; the launch traced here: 69.9 us
  Pallas kernels  69.8 us (100%)
    pallas_call x1, Pallas kernels, exchange(): pl.pallas_call(functools.partial(exchange_kernel, sizes), out_shape=(jax....  66.3 us
    pallas_call x1, Pallas kernels, apply_update(): pl.pallas_call(update_kernel, grid=(rows // tile,), out_shape=jax.ShapeDt...  3.52 us

profile of v5, /device:TPU:96, one launch (start us, length us, event | category | flops | bytes accessed | tf_op | source)
XLA Modules:
  0.0 69.9 jit_solution(6643395925097326224)
XLA Ops:
  0.0 0.0 copy-start
  0.0 66.3 %exchange.1 = (bf16[512,1792]{1,0:T(8,128)(2,1)S(1)}, bf16[1024,256]{1,0:T(8,128)(2,1)S(1)}) custom-call(bf16[4096,1792]{1,0:T(8,128)(2,1)} %quant_ref.1, s32[14,4096]{1,0:T(8,128)} %bitcast.2, bf16[1024,1792]{1,0:T(8,128)(2,1)} %weights_ref.3, s32[1024,256]{1,0:T(8,128)} %keep_ref.1), custom_call_target="tpu_custom_call" | custom-call | tf_op jit(solution)/shard_map/exchange/pallas_call | solution.py:533
  66.3 0.0 copy-done
  66.3 3.5 %update.1 = bf16[1024,1792]{1,0:T(8,128)(2,1)} custom-call(s32[1]{0:T(128)} %bitcast.feat_ref, bf16[512,1792]{1,0:T(8,128)(2,1)S(1)} %get-tuple-element.7.product_ref, bf16[1024,256]{1,0:T(8,128)(2,1)S(1)} %get-tuple-element.8.error_ref, bf16[1024,1792]{1,0:T(8,128)(2,1)S(1)} %copy-done), custom_call_target="tpu_custom_call" | custom-call | tf_op jit(solution)/shard_map/update/pallas_call | solution.py:584
Async XLA Ops:
  0.0 66.3 %copy-start = (bf16[1024,1792]{1,0:T(8,128)(2,1)S(1)}, bf16[1024,1792]{1,0:T(8,128)(2,1)}, u32[]{:S(2)}) copy-start(bf16[1024,1792]{1,0:T(8,128)(2,1)} %weights_ref.3) | copy-start | bytes 11010052
